TPU v7x, 32 devices: a whole 2x2x4 slice. The times are simulated.
32 devices in a mesh: dp: 16 (over z, y, core), tensor: 2 (over x).
Axes of the slice: x: 2, y: 2, z: 4, core: 2. Of those that a mesh axis runs over, the one named last changes fastest.
Arguments:
- tokens: bfloat16 [81920, 1024], P(('dp', 'tensor')), may hold values from -6 to 6
- kept: int32 [256], P('dp'), may hold values from 180 to 256
- cotangent: bfloat16 [81920, 1024], P(('dp', 'tensor')), may hold values from -6 to 6
- w_qkv: bfloat16 [3, 1024, 1024], P(None, 'dp', 'tensor'), may hold values from -0.1875 to 0.1875
- w_out: bfloat16 [1024, 1024], P('tensor', 'dp'), may hold values from -0.75 to 0.75
- w_up: bfloat16 [1024, 4096], P('dp', 'tensor'), may hold values from -0.1875 to 0.1875
- w_down: bfloat16 [4096, 1024], P('tensor', 'dp'), may hold values from -0.09375 to 0.09375
- qv_bias: bfloat16 [2, 1024], P(None, ('tensor', 'dp')), may hold values from -3 to 3
- up_bias: bfloat16 [4096], P(('tensor', 'dp')), may hold values from -3 to 3
- ln_gain: float32 [2, 1024], P(None, ('dp', 'tensor')), may hold values from 0.5 to 1.5
- shift: float32 [4, 1024], P(None, ('dp', 'tensor')), may hold values from -3 to 3
Outputs:
- layer_out: bfloat16 [81920, 1024], P(('dp', 'tensor'))
- grad_tokens: float32 [81920, 1024], P(('dp', 'tensor'))
- grad_qkv: float32 [3, 1024, 1024], P(None, 'dp', 'tensor')
- grad_out: float32 [1024, 1024], P('tensor', 'dp')
- grad_up: float32 [1024, 4096], P('dp', 'tensor')
- grad_down: float32 [4096, 1024], P('tensor', 'dp')
- grad_qv_bias: float32 [2, 1024], P(None, ('tensor', 'dp'))
- grad_up_bias: float32 [4096], P(('tensor', 'dp'))
- grad_gain: float32 [2, 1024], P(None, ('dp', 'tensor'))
- grad_shift: float32 [4, 1024], P(None, ('dp', 'tensor'))
Inputs may be any that keep to these rules, and one draw needn't show every extreme that they name: kept patches of each image; an image's first 64 tokens and its first kept patch tokens are valid, the rest of its 320 tokens are padding.
All inputs are finite; a program needn't handle non-finite values.
Results may differ from a plain program's by a relative error of at most 0.02.
Values may be sent and summed in bfloat16 or wider, within the bound.
No kernel may reach another device: no remote copies, remote signals or barrier semaphores. Data moves between devices by JAX's collectives and lax.ppermute only.
A program may use at most 320 MiB of HBM per device.

v0:
```python
import jax
import jax.numpy as jnp
from jax import lax
from jax.sharding import PartitionSpec as P

HEAD_DIM = 64
BUFFER = 64
SEQ = 320
EPSILON = 1e-06
NEGATIVE = -1000000000.0


def times_flip(left, right):
    return lax.dot_general(
        left, right, (((1,), (1,)), ((), ())), preferred_element_type=jnp.float32
    )


def inner_rows(left, right):
    return lax.dot_general(
        left, right, (((0,), (0,)), ((), ())), preferred_element_type=jnp.float32
    )


def norm_parts(values):
    centred = values - jnp.mean(values, axis=-1, keepdims=True)
    inverse = lax.rsqrt(jnp.mean(centred * centred, axis=-1, keepdims=True) + EPSILON)
    return (centred * inverse, inverse)


def norm_back(grad_normed, normed, inverse):
    first = jnp.mean(grad_normed, axis=-1, keepdims=True)
    second = jnp.mean(grad_normed * normed, axis=-1, keepdims=True)
    return inverse * (grad_normed - first - normed * second)


def gelu_tanh(values):
    return jax.nn.gelu(values, approximate=True)


def fetch_params(w_qkv, w_out, w_up, w_down, qv_bias, up_bias):
    part_qkv, part_out, part_up, part_down, part_qv, part_bias = (
        lax.all_gather(w_qkv, "dp", axis=1, tiled=True),
        lax.all_gather(w_out, "dp", axis=1, tiled=True),
        lax.all_gather(w_up, "dp", axis=0, tiled=True),
        lax.all_gather(w_down, "dp", axis=1, tiled=True),
        lax.all_gather(qv_bias, "dp", axis=1, tiled=True),
        lax.all_gather(up_bias, "dp", axis=0, tiled=True),
    )
    return (part_qkv, part_out, part_up, part_down, part_qv, part_bias)


def narrow_mlp(grad_up, grad_down, grad_bias_up):
    return (grad_up, grad_down, grad_bias_up)


def narrow_attn(grad_qkv, grad_out, grad_qv_bias):
    return (grad_qkv, grad_out, grad_qv_bias)


def gather_acts(values):
    return lax.all_gather(values, "tensor", axis=0, tiled=True)


def gather_grads(values):
    return lax.all_gather(values, "tensor", axis=0, tiled=True)


def sum_forward(left, right, rows):

    def term(start, count):
        return jnp.dot(left, right, preferred_element_type=jnp.float32)

    return lax.psum_scatter(
        term(jnp.int32(0), rows * lax.axis_size("tensor")).astype(jnp.bfloat16),
        "tensor",
        scatter_dimension=0,
        tiled=True,
    ).astype(jnp.float32)


def sum_backward(lefts, rights, rows):

    def term(start, count):
        total = None
        for left, right in zip(lefts, rights):
            part = times_flip(left, right)
            total = part if total is None else total + part
        return total

    return lax.psum_scatter(
        term(jnp.int32(0), rows * lax.axis_size("tensor")),
        "tensor",
        scatter_dimension=0,
        tiled=True,
    )


def scores_of(query, key, keep):
    scores = jnp.einsum(
        "bqhe,bkhe->bhqk", query, key, preferred_element_type=jnp.float32
    ) * HEAD_DIM ** (-0.5)
    return jnp.where(keep[:, None, None, :] > 0.5, scores, NEGATIVE)


def attend(block):
    query, key, value, keep = block
    scores = scores_of(query, key, keep)
    highest = jnp.max(scores, axis=-1, keepdims=True)
    expo = jnp.exp(scores - highest)
    denom = jnp.sum(expo, axis=-1, keepdims=True)
    probs = (expo / denom).astype(jnp.bfloat16)
    result = jnp.einsum("bhqk,bkhe->bqhe", probs, value, preferred_element_type=jnp.float32)
    return (result.astype(jnp.bfloat16), (highest + jnp.log(denom))[..., 0])


def attend_back(block):
    query, key, value, keep, logsum, grad_attn = block
    scores = scores_of(query, key, keep)
    probs = jnp.exp(scores - logsum[..., None])
    grad_probs = jnp.einsum("bqhe,bkhe->bhqk", grad_attn, value, preferred_element_type=jnp.float32)
    grad_scores = probs * (grad_probs - jnp.sum(probs * grad_probs, axis=-1, keepdims=True))
    grad_scores = grad_scores.astype(jnp.bfloat16)
    scale = HEAD_DIM ** (-0.5)
    grad_query = (
        jnp.einsum("bhqk,bkhe->bqhe", grad_scores, key, preferred_element_type=jnp.float32) * scale
    )
    grad_key = (
        jnp.einsum("bhqk,bqhe->bkhe", grad_scores, query, preferred_element_type=jnp.float32)
        * scale
    )
    grad_value = jnp.einsum(
        "bhqk,bqhe->bkhe", probs.astype(jnp.bfloat16), grad_attn, preferred_element_type=jnp.float32
    )
    return (
        grad_query.astype(jnp.bfloat16),
        grad_key.astype(jnp.bfloat16),
        grad_value.astype(jnp.bfloat16),
    )


def body(tokens, kept, cotangent, w_qkv, w_out, w_up, w_down, qv_bias, up_bias, ln_gain, shift):
    rows = tokens.shape[0]
    full_qkv, full_out, full_up, full_down, bias_qv, bias_up = fetch_params(
        w_qkv, w_out, w_up, w_down, qv_bias, up_bias
    )
    gain, shifts = (
        lax.all_gather(ln_gain, ("dp", "tensor"), axis=1, tiled=True),
        lax.all_gather(shift, ("dp", "tensor"), axis=1, tiled=True),
    )
    heads = full_qkv.shape[2] // HEAD_DIM
    width = heads * HEAD_DIM
    positions = jnp.arange(SEQ, dtype=jnp.int32)
    images = kept.shape[0]
    keep = (positions[None, :] < BUFFER + kept[:, None]).astype(jnp.float32)
    group = images * SEQ
    offset = lax.axis_index("tensor") * rows
    keep_own = lax.dynamic_slice_in_dim(keep.reshape(group), offset, rows, 0)[:, None]
    pairs = images // 2
    keep_pairs = keep.reshape(pairs, 2, SEQ)
    x_values = tokens.astype(jnp.float32)
    normed1, inverse1 = norm_parts(x_values)
    h1_all = gather_acts((normed1 * gain[0] + shifts[0]).astype(jnp.bfloat16))
    bias_float = bias_qv.astype(jnp.float32)
    bias_rows = jnp.stack([bias_float[0], jnp.zeros_like(bias_float[0]), bias_float[1]])
    projected = jnp.einsum("rd,kdc->krc", h1_all, full_qkv, preferred_element_type=jnp.float32)
    qkv = (projected + bias_rows[:, None, :]).astype(jnp.bfloat16)
    split_shape = (pairs, 2, SEQ, heads, HEAD_DIM)
    query = qkv[0].reshape(split_shape)
    key = qkv[1].reshape(split_shape)
    value = qkv[2].reshape(split_shape)
    attn_blocks, logsum = lax.map(attend, (query, key, value, keep_pairs))
    attn = attn_blocks.reshape(group, width)
    mixed = x_values + sum_forward(attn, full_out, rows) + shifts[2]
    normed2, inverse2 = norm_parts(mixed)
    h2_all = gather_acts((normed2 * gain[1] + shifts[1]).astype(jnp.bfloat16))
    pre = jnp.dot(h2_all, full_up, preferred_element_type=jnp.float32) + bias_up.astype(jnp.float32)
    activated, gelu_pull = jax.vjp(gelu_tanh, pre)
    activated = activated.astype(jnp.bfloat16)
    result = (mixed + sum_forward(activated, full_down, rows) + shifts[3]) * keep_own
    layer_out = result.astype(jnp.bfloat16)
    full_qkv, full_out, full_up, full_down, spare_qv, spare_up = fetch_params(
        w_qkv, w_out, w_up, w_down, qv_bias, up_bias
    )
    grad = cotangent.astype(jnp.float32) * keep_own
    grad_m_all = gather_grads(grad.astype(jnp.bfloat16))
    grad_down = inner_rows(activated, grad_m_all)
    grad_pre = gelu_pull(times_flip(grad_m_all, full_down))[0].astype(jnp.bfloat16)
    grad_bias_up = jnp.sum(grad_pre, axis=0, dtype=jnp.float32)
    grad_up = inner_rows(h2_all, grad_pre)
    grad_up, grad_down, grad_bias_up = narrow_mlp(grad_up, grad_down, grad_bias_up)
    grad_h2 = sum_backward((grad_pre,), (full_up,), rows)
    grad_mixed = grad + norm_back(grad_h2 * gain[1], normed2, inverse2)
    grad_o_all = gather_grads(grad_mixed.astype(jnp.bfloat16))
    grad_out = inner_rows(attn, grad_o_all)
    grad_attn = times_flip(grad_o_all, full_out).astype(jnp.bfloat16).reshape(split_shape)
    grad_query, grad_key, grad_value = lax.map(
        attend_back, (query, key, value, keep_pairs, logsum, grad_attn)
    )
    grad_query = grad_query.reshape(group, width)
    grad_key = grad_key.reshape(group, width)
    grad_value = grad_value.reshape(group, width)
    stacked = jnp.stack([grad_query, grad_key, grad_value])
    grad_qkv = jnp.einsum("rd,krc->kdc", h1_all, stacked, preferred_element_type=jnp.float32)
    grad_qv_bias = jnp.stack(
        [
            jnp.sum(grad_query, axis=0, dtype=jnp.float32),
            jnp.sum(grad_value, axis=0, dtype=jnp.float32),
        ]
    )
    grad_h1 = sum_backward(
        (grad_query, grad_key, grad_value), (full_qkv[0], full_qkv[1], full_qkv[2]), rows
    )
    grad_tokens = grad_mixed + norm_back(grad_h1 * gain[0], normed1, inverse1)
    grad_qkv, grad_out, grad_qv_bias = narrow_attn(grad_qkv, grad_out, grad_qv_bias)
    sent_qkv, sent_out, sent_up, sent_down, sent_qv_bias, sent_bias_up = (
        lax.psum_scatter(
            grad_qkv.astype(jnp.bfloat16), "dp", scatter_dimension=1, tiled=True
        ).astype(jnp.float32),
        lax.psum_scatter(
            grad_out.astype(jnp.bfloat16), "dp", scatter_dimension=1, tiled=True
        ).astype(jnp.float32),
        lax.psum_scatter(
            grad_up.astype(jnp.bfloat16), "dp", scatter_dimension=0, tiled=True
        ).astype(jnp.float32),
        lax.psum_scatter(
            grad_down.astype(jnp.bfloat16), "dp", scatter_dimension=1, tiled=True
        ).astype(jnp.float32),
        lax.psum_scatter(
            grad_qv_bias.astype(jnp.bfloat16), "dp", scatter_dimension=1, tiled=True
        ).astype(jnp.float32),
        lax.psum_scatter(
            grad_bias_up.astype(jnp.bfloat16), "dp", scatter_dimension=0, tiled=True
        ).astype(jnp.float32),
    )
    grad_gain = jnp.stack([jnp.sum(grad_h1 * normed1, axis=0), jnp.sum(grad_h2 * normed2, axis=0)])
    grad_shift = jnp.stack(
        [
            jnp.sum(grad_h1, axis=0),
            jnp.sum(grad_h2, axis=0),
            jnp.sum(grad_mixed, axis=0),
            jnp.sum(grad, axis=0),
        ]
    )
    sent_gain, sent_shift = (
        lax.psum_scatter(grad_gain, ("dp", "tensor"), scatter_dimension=1, tiled=True),
        lax.psum_scatter(grad_shift, ("dp", "tensor"), scatter_dimension=1, tiled=True),
    )
    return (
        layer_out,
        grad_tokens,
        sent_qkv,
        sent_out,
        sent_up,
        sent_down,
        sent_qv_bias,
        sent_bias_up,
        sent_gain,
        sent_shift,
    )


def solution(mesh):
    return jax.shard_map(
        body,
        mesh=mesh,
        in_specs=(
            P(("dp", "tensor"), None),
            P("dp"),
            P(("dp", "tensor"), None),
            P(None, "dp", "tensor"),
            P("tensor", "dp"),
            P("dp", "tensor"),
            P("tensor", "dp"),
            P(None, ("tensor", "dp")),
            P(("tensor", "dp")),
            P(None, ("dp", "tensor")),
            P(None, ("dp", "tensor")),
        ),
        out_specs=(
            P(("dp", "tensor"), None),
            P(("dp", "tensor"), None),
            P(None, "dp", "tensor"),
            P("tensor", "dp"),
            P("dp", "tensor"),
            P("tensor", "dp"),
            P(None, ("tensor", "dp")),
            P(("tensor", "dp")),
            P(None, ("dp", "tensor")),
            P(None, ("dp", "tensor")),
        ),
        check_vma=False,
    )
```

profile of v0, /device:TPU:0, one launch (start us, length us, event | category | flops | bytes accessed | tf_op | source)
XLA Modules:
  0.0 2642.8 jit_solution(9621192983766315646)
XLA Ops:
  8.0 70.4 %all-gather = f32[32,32,2]{1,2,0:T(2,128)S(1)} all-gather(f32[1,32,2]{1,2,0:T(2,128)} %bitcast.235), channel_id=1, replica_groups=mesh['dp'=16,'tensor'=2] {'dp','tensor'}, dimensions={0}, use_global_device_ids=true | all-gather | bytes 8448 | tf_op jit(solution)/shard_map/all_gather | solution.py:148
  78.4 63.9 %all-gather.1 = f32[32,32,4]{1,2,0:T(4,128)S(1)} all-gather(f32[1,32,4]{1,2,0:T(4,128)} %bitcast.234), channel_id=1, replica_groups=mesh['dp'=16,'tensor'=2] {'dp','tensor'}, dimensions={0}, use_global_device_ids=true | all-gather | bytes 16896 | tf_op jit(solution)/shard_map/all_gather | solution.py:149
  154.2 17.3 all-gather.2
  171.8 108.7 %all-gather.13.cloned.1.call-done = bf16[5120,1024]{1,0:T(8,128)(2,1)} async-done(((bf16[2560,1024]{1,0:T(8,128)(2,1)}), bf16[5120,1024]{1,0:T(8,128)(2,1)}) %all-gather.13.cloned.1.call-update) | async-done | bytes 10485776 | tf_op jit(solution)/shard_map/all_gather | solution.py:62
  280.4 19.9 fusion.62
  306.3 13.9 reshape.173
  320.2 12.6 copy.101
  332.8 13.9 reshape.172
  346.7 12.7 copy.100
  359.3 13.9 reshape.171
  373.2 12.8 copy.99
  392.0 88.5 %while.26 = (s32[]{:T(128)}, bf16[8,2,320,8,64]{2,1,0,4,3:T(2,128)(2,1)}, f32[8,2,8,320]{3,2,1,0:T(8,128)}, bf16[8,2,320,8,64]{2,4,3,1,0:T(8,128)(2,1)}, f32[8,2...) while((s32[]{:T(128)}, ...), condition=%wide.region_5.6_spmd, body=%wide.region_2.5_spmd.sunk | while | flops 439414400 | bytes 24291436 | solution.py:172
  480.5 14.3 reshape.145
  506.8 121.5 %reduce-scatter.17.cloned.1.call-done = bf16[2560,1024]{1,0:T(8,128)(2,1)} async-done(((bf16[5120,1024]{1,0:T(8,128)(2,1)}), bf16[2560,1024]{1,0:T(8,128)(2,1)}) %reduce-scatter.17.cloned.1.call-update) | async-done | bytes 5242896 | tf_op jit(solution)/shard_map/reduce_scatter | solution.py:74
  651.4 21.7 all-gather.3
  680.9 130.0 %all-gather.19.cloned.1.call-done = bf16[5120,1024]{1,0:T(8,128)(2,1)} async-done(((bf16[2560,1024]{1,0:T(8,128)(2,1)}), bf16[5120,1024]{1,0:T(8,128)(2,1)}) %all-gather.19.cloned.1.call-update) | async-done | bytes 10485776 | tf_op jit(solution)/shard_map/all_gather | solution.py:62
  810.9 42.1 %multiply_convert_fusion.3 = (bf16[5120,2048]{1,0:T(8,128)(2,1)}, f32[5120,2048]{1,0:T(8,128)}) fusion(f32[2048]{0:T(1024)S(1)} %bitcast.232, bf16[5120,1024]{1,0:T(8,128)(2,1)} %all-gather.19.cloned.1.call-done, bf16[1024,2048]{1,0:T(8,128)(2,1)} %all-gather.21.cloned.1.call-done), kind=kOutput, calls=%fused_computation.71 | convolution fusion | flops 21579694080 | bytes 77602816 | tf_op jit(solution)/shard_map/dot_general | solution.py:177
  863.5 130.2 %all-gather.25.cloned.1.call-done = bf16[5120,1024]{1,0:T(8,128)(2,1)} async-done(((bf16[2560,1024]{1,0:T(8,128)(2,1)}), bf16[5120,1024]{1,0:T(8,128)(2,1)}) %all-gather.25.cloned.1.call-update) | async-done | bytes 10485776 | tf_op jit(solution)/shard_map/all_gather | solution.py:66
  993.6 56.0 %fusion.102 = (bf16[2048]{0:T(1024)(128)(2,1)}, bf16[5120,2048]{1,0:T(8,128)(2,1)}) fusion(f32[5120,2048]{1,0:T(8,128)} %get-tuple-element.277, f32[2048]{0:T(1024)S(1)} %bitcast.233, bf16[5120,1024]{1,0:T(8,128)(2,1)} %all-gather.25.cloned.1.call-done, bf16[2048,1024]{0,1:T(8,128)(2,1)} %all-gather.23.cloned.1.call-done), kind=kOutput, calls=%fused_computation.151 | convolution fusion | flops 21705521152 | bytes 77606912 | tf_op jit(solution)/shard_map/dot_general | solution.py:14
  1049.7 28.5 %fusion.103 = f32[5120,1024]{1,0:T(8,128)} fusion(bf16[5120,2048]{1,0:T(8,128)(2,1)} %get-tuple-element.279, bf16[1024,2048]{1,0:T(8,128)(2,1)} %all-gather.21.cloned.1.call-done), kind=kOutput, calls=%fused_computation.152 | convolution fusion | flops 21474836480 | bytes 46137344 | tf_op jit(solution)/shard_map/dot_general | solution.py:14
  1078.3 27.9 %convolution_convert_fusion.1 = bf16[5120,1024]{1,0:T(8,128)(2,1)} fusion(bf16[5120,2048]{1,0:T(8,128)(2,1)} %get-tuple-element.276, bf16[2048,1024]{0,1:T(8,128)(2,1)} %all-gather.23.cloned.1.call-done), kind=kOutput, calls=%fused_computation.112 | convolution fusion | flops 21480079360 | bytes 35651584 | tf_op jit(solution)/shard_map/dot_general | solution.py:72
  1106.2 206.4 %reduce-scatter.21.cloned.1.call-done = f32[2560,1024]{1,0:T(8,128)} async-done(((f32[5120,1024]{1,0:T(8,128)}), f32[2560,1024]{1,0:T(8,128)}) %reduce-scatter.21.cloned.1.call-update) | async-done | bytes 10485776 | tf_op jit(solution)/shard_map/reduce_scatter | solution.py:91
  1323.4 114.0 %reduce-scatter.19.cloned.1.call-done = bf16[2560,1024]{1,0:T(8,128)(2,1)} async-done(((bf16[5120,1024]{1,0:T(8,128)(2,1)}), bf16[2560,1024]{1,0:T(8,128)(2,1)}) %reduce-scatter.19.cloned.1.call-update) | async-done | bytes 5242896 | tf_op jit(solution)/shard_map/reduce_scatter | solution.py:74
  1437.4 16.5 fusion.97
  1461.2 29.1 %convolution_convert_fusion.3 = bf16[2048,1024]{0,1:T(8,128)(2,1)} fusion(bf16[5120,2048]{1,0:T(8,128)(2,1)} %get-tuple-element.276, bf16[5120,1024]{1,0:T(8,128)(2,1)} %all-gather.25.cloned.1.call-done), kind=kOutput, calls=%fused_computation.116 | convolution fusion | flops 21476933632 | bytes 35651584 | tf_op jit(solution)/shard_map/dot_general | solution.py:20
  1490.4 29.3 %convolution_convert_fusion.4 = bf16[1024,2048]{1,0:T(8,128)(2,1)} fusion(bf16[5120,1024]{1,0:T(8,128)(2,1)} %all-gather.19.cloned.1.call-done, bf16[5120,2048]{1,0:T(8,128)(2,1)} %get-tuple-element.279), kind=kOutput, calls=%fused_computation.117 | convolution fusion | flops 21476933632 | bytes 35651584 | tf_op jit(solution)/shard_map/dot_general | solution.py:20
  1519.8 71.1 %all-gather.27.cloned.1.call-done = bf16[5120,1024]{1,0:T(8,128)(2,1)} async-done(((bf16[2560,1024]{1,0:T(8,128)(2,1)}), bf16[5120,1024]{1,0:T(8,128)(2,1)}) %all-gather.27.cloned.1.call-update) | async-done | bytes 10485776 | tf_op jit(solution)/shard_map/all_gather | solution.py:66
  1602.1 14.0 reshape.162
  1616.1 12.7 copy.106
  1634.7 177.6 %while.27 = (s32[]{:T(128)}, bf16[8,2,320,8,64]{2,4,3,1,0:T(8,128)(2,1)}, bf16[8,2,320,8,64]{2,1,0,4,3:T(2,128)(2,1)}, bf16[8,2,320,8,64]{2,4,3,1,0:T(8,128)(2,1...) while((s32[]{:T(128)}, ...), condition=%wide.region_15.16_spmd, body=%wide.region_13.15_spmd.sunk | while | flops 1074785920 | bytes 58479748 | solution.py:197
  1812.3 12.7 copy.110
  1828.9 12.9 copy.108
  1846.6 14.3 stack_reshape.9
  1860.8 14.3 stack_reshape.11
  1875.1 14.3 stack_reshape.10
  1889.5 22.5 convert_bitcast_fusion
  1917.8 14.5 reshape.147
  1932.3 14.3 reshape.149
  1946.6 14.4 reshape.148
  1972.1 13.0 fusion.93
  1985.0 12.6 fusion.94
  1997.7 23.9 add_add_fusion
  2024.1 34.6 %all-reduce.1 = bf16[2048]{0:T(1024)(128)(2,1)S(1)} all-reduce(bf16[2048]{0:T(1024)(128)(2,1)S(1)} %copy-done.27), channel_id=11, replica_groups=mesh['dp'=16,'tensor'=2] {'dp'}, use_global_device_ids=true, to_apply=%region_27.28.clone | all-reduce | flops 2048 | bytes 8192
  2066.0 53.7 %reduce-scatter.25.cloned.1.call-done = bf16[512,64]{0,1:T(8,128)(2,1)} async-done(((bf16[512,1024]{0,1:T(8,128)(2,1)}), bf16[512,64]{0,1:T(8,128)(2,1)}) %reduce-scatter.25.cloned.1.call-update) | async-done | bytes 65552 | tf_op jit(solution)/shard_map/reduce_scatter | solution.py:220
  2121.3 233.9 %reduce-scatter.23.cloned.1.call-done = f32[2560,1024]{1,0:T(8,128)} async-done(((f32[5120,1024]{1,0:T(8,128)}), f32[2560,1024]{1,0:T(8,128)}) %reduce-scatter.23.cloned.1.call-update) | async-done | bytes 10485776 | tf_op jit(solution)/shard_map/reduce_scatter | solution.py:91
  2365.5 14.1 fusion.80
  2379.6 120.8 %reduce-scatter.33.cloned.1.call-done = f32[32,2]{1,0:T(8,128)} async-done(((f32[1024,2]{1,0:T(8,128)}), f32[32,2]{1,0:T(8,128)}) %reduce-scatter.33.cloned.1.call-update) | async-done | bytes 272
  2501.7 132.9 %reduce-scatter.35.cloned.1.call-done = f32[32,4]{1,0:T(8,128)} async-done(((f32[1024,4]{1,0:T(8,128)}), f32[32,4]{1,0:T(8,128)}) %reduce-scatter.35.cloned.1.call-update) | async-done | bytes 528
  (307 shorter events, 427.2 us)
Async XLA Ops:
  7.2 164.6 %all-gather.15.cloned.1.call-start = ((), (), s32[]{:S(2)}) async-start(), calls=%async_computation.11 | async-start | bytes 3342336 | tf_op jit(solution)/shard_map/all_gather | solution.py:43
  7.9 272.5 %all-gather.13.cloned.1.call-start = ((), (), s32[]{:S(2)}) async-start(), calls=%async_computation.10 | async-start | bytes 15728640 | tf_op jit(solution)/shard_map/all_gather | solution.py:62
  142.5 4.2 copy-start
  143.1 5.8 copy-start.17
  148.2 5.5 copy-start.33
  148.2 6.0 copy-start.30
  152.8 341.9 %all-gather.17.cloned.1.call-start = ((), (), s32[]{:S(2)}) async-start(), calls=%async_computation.12 | async-start | bytes 1114112 | tf_op jit(solution)/shard_map/all_gather | solution.py:44
  153.6 474.7 %reduce-scatter.17.cloned.1.call-start = ((), (), s32[]{:S(2)}) async-start(), calls=%async_computation.13 | async-start | bytes 15728640 | tf_op jit(solution)/shard_map/reduce_scatter | solution.py:74
  480.4 25.7 copy-start.14
  506.1 122.1 %copy-start.12 = (f32[1,1024]{1,0:T(1,128)S(1)}, f32[1,1024]{1,0:T(1,128)}, u32[]{:S(2)}) copy-start(f32[1,1024]{1,0:T(1,128)} %get-tuple-element.270) | copy-start | bytes 12292
  506.1 128.1 %slice-start = ((s8[5242880]{0:T(1024)(128)(4,1)}), s8[1048576]{0:T(1024)(128)(4,1)S(1)}, s32[]{:S(2)}) async-start(s8[5242880]{0:T(1024)(128)(4,1)} %bitcast.201), calls=%async_computation.29 | async-start | bytes 2097152
  506.2 174.7 %all-gather.21.cloned.1.call-start = ((), (), s32[]{:S(2)}) async-start(), calls=%async_computation.15 | async-start | bytes 4456448 | tf_op jit(solution)/shard_map/all_gather | solution.py:45
  506.7 304.1 %all-gather.19.cloned.1.call-start = ((), (), s32[]{:S(2)}) async-start(), calls=%async_computation.14 | async-start | bytes 15728640 | tf_op jit(solution)/shard_map/all_gather | solution.py:62
  628.2 6.0 copy-start.1
  628.2 6.8 slice-start.1
  628.3 11.0 copy-start.19
  628.3 11.0 copy-start.23
  639.2 5.5 copy-start.29
  643.9 7.5 copy-start.31
  643.9 219.6 %all-gather.23.cloned.1.call-start = ((), (), s32[]{:S(2)}) async-start(), calls=%async_computation.16 | async-start | bytes 4456448 | tf_op jit(solution)/shard_map/all_gather | solution.py:46
  644.6 349.0 %all-gather.25.cloned.1.call-start = ((), (), s32[]{:S(2)}) async-start(), calls=%async_computation.18 | async-start | bytes 15728640 | tf_op jit(solution)/shard_map/all_gather | solution.py:66
  651.3 661.4 %reduce-scatter.21.cloned.1.call-start = ((), (), s32[]{:S(2)}) async-start(), calls=%async_computation.19 | async-start | bytes 31457280 | tf_op jit(solution)/shard_map/reduce_scatter | solution.py:91
  1078.2 359.2 %reduce-scatter.19.cloned.1.call-start = ((), (), s32[]{:S(2)}) async-start(), calls=%async_computation.17 | async-start | bytes 15728640 | tf_op jit(solution)/shard_map/reduce_scatter | solution.py:74
  1106.1 206.6 %copy-start.7 = (f32[2560]{0:T(1024)S(1)}, f32[2560]{0:T(1024)}, u32[]{:S(2)}) copy-start(f32[2560]{0:T(1024)} %copy-done.6) | copy-start | bytes 30724
  1106.1 206.6 %copy-start.11 = (f32[2560]{0:T(1024)S(1)}, f32[2560]{0:T(1024)}, u32[]{:S(2)}) copy-start(f32[2560]{0:T(1024)} %copy-done.10) | copy-start | bytes 30724
  1106.1 206.6 %copy-start.13 = (f32[1,1024]{1,0:T(1,128)S(1)}, f32[1,1024]{1,0:T(1,128)}, u32[]{:S(2)}) copy-start(f32[1,1024]{1,0:T(1,128)} %get-tuple-element.270) | copy-start | bytes 12292
  1106.1 206.6 %copy-start.20 = (f32[1,1024]{1,0:T(1,128)S(1)}, f32[1,1024]{1,0:T(1,128)}, u32[]{:S(2)}) copy-start(f32[1,1024]{1,0:T(1,128)} %get-tuple-element.273) | copy-start | bytes 12292
  1106.2 331.2 %copy-start.16 = (f32[2560]{0:T(1024)S(1)}, f32[2560]{0:T(1024)}, u32[]{:S(2)}) copy-start(f32[2560]{0:T(1024)} %copy-done.15) | copy-start | bytes 30724
  1106.2 331.2 %copy-start.26 = (f32[1,1024]{1,0:T(1,128)S(1)}, f32[1,1024]{1,0:T(1,128)}, u32[]{:S(2)}) copy-start(f32[1,1024]{1,0:T(1,128)} %get-tuple-element.268) | copy-start | bytes 12292
  1106.2 484.6 %all-gather.27.cloned.1.call-start = ((), (), s32[]{:S(2)}) async-start(), calls=%async_computation.20 | async-start | bytes 15728640 | tf_op jit(solution)/shard_map/all_gather | solution.py:66
  1453.9 4.1 copy-start.2
  1461.2 598.1 %reduce-scatter.29.cloned.1.call-start = ((), (), s32[]{:S(2)}) async-start(), calls=%async_computation.24 | async-start | bytes 4456448 | tf_op jit(solution)/shard_map/reduce_scatter | solution.py:226
  1490.3 570.7 %reduce-scatter.27.cloned.1.call-start = ((), (), s32[]{:S(2)}) async-start(), calls=%async_computation.23 | async-start | bytes 4456448 | tf_op jit(solution)/shard_map/reduce_scatter | solution.py:223
  1490.4 100.4 %copy-start.32 = (bf16[512,1024]{0,1:T(8,128)(2,1)S(1)}, bf16[512,1024]{0,1:T(8,128)(2,1)}, u32[]{:S(2)}) copy-start(bf16[512,1024]{0,1:T(8,128)(2,1)} %all-gather.17.cloned.1.call-done) | copy-start | bytes 3145732
  1519.7 543.1 %reduce-scatter.31.cloned.1.call-start = ((), (), s32[]{:S(2)}) async-start(), calls=%async_computation.25 | async-start | bytes 139264
  1889.5 174.7 %all-reduce.4.cloned.1.call-start = ((), (), s32[]{:S(2)}) async-start(), calls=%async_computation.28 | async-start | bytes 8388608
  1917.8 202.0 %reduce-scatter.25.cloned.1.call-start = ((), (), s32[]{:S(2)}) async-start(), calls=%async_computation.22 | async-start | bytes 1114112 | tf_op jit(solution)/shard_map/reduce_scatter | solution.py:220
  1961.0 11.0 copy-start.3
  1972.0 383.2 %reduce-scatter.23.cloned.1.call-start = ((), (), s32[]{:S(2)}) async-start(), calls=%async_computation.21 | async-start | bytes 31457280 | tf_op jit(solution)/shard_map/reduce_scatter | solution.py:91
  2021.6 333.7 %copy-start.5 = (f32[2560]{0:T(1024)S(1)}, f32[2560]{0:T(1024)}, u32[]{:S(2)}) copy-start(f32[2560]{0:T(1024)} %copy-done.4) | copy-start | bytes 30724
  2021.6 333.7 %copy-start.9 = (f32[2560]{0:T(1024)S(1)}, f32[2560]{0:T(1024)}, u32[]{:S(2)}) copy-start(f32[2560]{0:T(1024)} %copy-done.8) | copy-start | bytes 30724
  2021.6 333.7 %copy-start.18 = (f32[1,1024]{1,0:T(1,128)S(1)}, f32[1,1024]{1,0:T(1,128)}, u32[]{:S(2)}) copy-start(f32[1,1024]{1,0:T(1,128)} %copy-done.17) | copy-start | bytes 12292
  2021.6 478.8 %reduce-scatter.33.cloned.1.call-start = ((), (), s32[]{:S(2)}) async-start(), calls=%async_computation.26 | async-start | bytes 540672
  2065.2 298.1 %copy-start.21 = (f32[1024]{0:T(1024)S(1)}, f32[1024]{0:T(1024)}, u32[]{:S(2)}) copy-start(f32[1024]{0:T(1024)} %get-tuple-element.215) | copy-start | bytes 12292
  2121.3 243.1 %copy-start.22 = (f32[1024]{0:T(1024)S(1)}, f32[1024]{0:T(1024)}, u32[]{:S(2)}) copy-start(f32[1024]{0:T(1024)} %get-tuple-element.222) | copy-start | bytes 12292
  2121.3 243.1 %copy-start.24 = (f32[1024]{0:T(1024)S(1)}, f32[1024]{0:T(1024)}, u32[]{:S(2)}) copy-start(f32[1024]{0:T(1024)} %get-tuple-element.257) | copy-start | bytes 12292
  2121.3 243.1 %copy-start.25 = (f32[1024]{0:T(1024)S(1)}, f32[1024]{0:T(1024)}, u32[]{:S(2)}) copy-start(f32[1024]{0:T(1024)} %get-tuple-element.267) | copy-start | bytes 12292
  2364.4 270.3 %reduce-scatter.35.cloned.1.call-start = ((), (), s32[]{:S(2)}) async-start(), calls=%async_computation.27 | async-start | bytes 540672
  (8 other events, 11.3 us)
Sparse Core Ops, SparseCore 0:
  10.2 48.2 all-gather.14
  153.0 127.4 all-gather.12
  282.6 37.8 all-gather.16
  506.3 121.9 reduce-scatter.16
  630.3 50.5 all-gather.20
  682.9 127.9 all-gather.18
  813.0 50.3 all-gather.22
  865.6 127.9 all-gather.24
  1078.3 234.2 reduce-scatter.20
  1315.4 121.9 reduce-scatter.18
  1461.3 129.4 all-gather.26
  1594.5 72.7 reduce-scatter.28
  1671.2 71.8 reduce-scatter.26
  1889.6 55.8 reduce-scatter.30
  1949.0 110.3 all-reduce.3
  2062.8 56.9 reduce-scatter.24
  2121.9 233.2 reduce-scatter.22
  2364.5 135.8 reduce-scatter.32
  2502.6 131.9 reduce-scatter.34
where the time goes:
time: 2650 us; the launch traced here: 2640 us
  waiting for transfers between devices  1440 us (54%)
  matrix products  525 us (20%)
  local copies, waits for them, and re-layouts  306 us (12%)
  blocking collectives  208 us (8%)
  other arithmetic  142 us (5%)
    reduce_scatter x2, waiting for transfers between devices, sum_backward(): lax.psum_scatter(term(jnp.int32(0), rows * lax.axis_size('tensor')), 'ten...  440 us
    unnamed x23, waiting for transfers between devices  257 us
    all_gather x2, waiting for transfers between devices, gather_acts(): return lax.all_gather(values, 'tensor', axis=0, tiled=True)  239 us
    reduce_scatter x2, waiting for transfers between devices, sum_forward(): lax.psum_scatter(term(jnp.int32(0), rows * lax.axis_size('tensor')).astyp...  235 us
    all_gather x2, waiting for transfers between devices, gather_grads(): return lax.all_gather(values, 'tensor', axis=0, tiled=True)  201 us
    dot_general x6, matrix products, times_flip(): lax.dot_general(left, right, (((1,), (1,)), ((), ())), preferred_element_...  145 us
    all_gather x1, blocking collectives, body(): lax.all_gather(ln_gain, ('dp', 'tensor'), axis=1, tiled=True)  70.4 us
    dot_general x3, matrix products, inner_rows(): lax.dot_general(left, right, (((0,), (0,)), ((), ())), preferred_element_...  69.3 us
  transfers between devices with their start and end apart: 19, of which 13 were waited for; matrix products, arithmetic and copies ran while one was open for 32% of the time, Pallas kernels for 0%

commit v1 on v0

--- a/solution.py
+++ b/solution.py
@@ -59,7 +59,9 @@
 
 
 def gather_acts(values):
-    return lax.all_gather(values, "tensor", axis=0, tiled=True)
+    return jnp.concatenate(
+        lax.all_to_all(jnp.stack([values] * lax.axis_size("tensor")), "tensor", 0, 0), axis=0
+    )
 
 
 def gather_grads(values):

time: 2650 us -> 2550 us (0.962)
  waiting for transfers between devices: 1440 us -> 1300 us
    all_gather x2 -> x0, waiting for transfers between devices: 239 us -> none  [gather_acts(): return lax.all_gather(values, 'tensor', axis=0, tiled=True)]
    all_to_all x0 -> x2, waiting for transfers between devices: none -> 209 us  [gather_acts(): lax.all_to_all(jnp.stack([values] * lax.axis_size('tensor')), 'tensor', 0...]
    all_gather x2, waiting for transfers between devices: 201 us -> 113 us  [gather_grads(): return lax.all_gather(values, 'tensor', axis=0, tiled=True)]
    another operation x2 -> x6, other arithmetic: 0.01 us -> 29.7 us  [the longest x4 29.7 us: gather_acts(): jnp.stack([values] * lax.axis_size('tensor'))]
    unnamed x23 -> x21, waiting for transfers between devices: 257 us -> 256 us
  transfers between devices with their start and end apart: 19 -> 19, of which waited for: 13 -> 11; matrix products, arithmetic and copies ran while one was open for 32% -> 34% of each run, Pallas kernels for 0% -> 0%
where the time goes in v1:
time: 2550 us; the launch traced here: 2540 us
  waiting for transfers between devices  1300 us (51%)
  matrix products  525 us (21%)
  local copies, waits for them, and re-layouts  306 us (12%)
  blocking collectives  207 us (8%)
  other arithmetic  165 us (6%)
    reduce_scatter x2, waiting for transfers between devices, sum_backward(): lax.psum_scatter(term(jnp.int32(0), rows * lax.axis_size('tensor')), 'ten...  440 us
    unnamed x21, waiting for transfers between devices  256 us
    reduce_scatter x2, waiting for transfers between devices, sum_forward(): lax.psum_scatter(term(jnp.int32(0), rows * lax.axis_size('tensor')).astyp...  231 us
    all_to_all x2, waiting for transfers between devices, gather_acts(): lax.all_to_all(jnp.stack([values] * lax.axis_size('tensor')), 'tensor', 0...  209 us
    dot_general x6, matrix products, times_flip(): lax.dot_general(left, right, (((1,), (1,)), ((), ())), preferred_element_...  145 us
    all_gather x2, waiting for transfers between devices, gather_grads(): return lax.all_gather(values, 'tensor', axis=0, tiled=True)  113 us
    all_gather x1, blocking collectives, body(): lax.all_gather(ln_gain, ('dp', 'tensor'), axis=1, tiled=True)  70.1 us
    dot_general x3, matrix products, inner_rows(): lax.dot_general(left, right, (((0,), (0,)), ((), ())), preferred_element_...  69.3 us
  transfers between devices with their start and end apart: 19, of which 11 were waited for; matrix products, arithmetic and copies ran while one was open for 34% of the time, Pallas kernels for 0%

profile of v1, /device:TPU:0, one launch (start us, length us, event | category | flops | bytes accessed | tf_op | source)
XLA Modules:
  0.0 2538.8 jit_solution(4083613759570185385)
XLA Ops:
  15.2 70.1 %all-gather = f32[32,32,2]{1,2,0:T(2,128)S(1)} all-gather(f32[1,32,2]{1,2,0:T(2,128)S(1)} %bitcast.238), channel_id=1, replica_groups=mesh['dp'=16,'tensor'=2] {'dp','tensor'}, dimensions={0}, use_global_device_ids=true | all-gather | bytes 8448 | tf_op jit(solution)/shard_map/all_gather | solution.py:150
  85.5 63.7 %all-gather.1 = f32[32,32,4]{1,2,0:T(4,128)S(1)} all-gather(f32[1,32,4]{1,2,0:T(4,128)S(1)} %bitcast.237), channel_id=1, replica_groups=mesh['dp'=16,'tensor'=2] {'dp','tensor'}, dimensions={0}, use_global_device_ids=true | all-gather | bytes 16896 | tf_op jit(solution)/shard_map/all_gather | solution.py:151
  175.5 17.6 all-gather.2
  193.4 93.3 %all-to-all-done = bf16[2,2560,1024]{2,1,0:T(8,128)(2,1)} async-done(((bf16[2,2560,1024]{2,1,0:T(8,128)(2,1)}), bf16[2,2560,1024]{2,1,0:T(8,128)(2,1)}, u32[]{:S(2)}, u32[]{:S(2)}) %all-to-all-start) | async-done | bytes 10485792 | tf_op jit(solution)/shard_map/all_to_all | solution.py:63
  286.8 19.9 fusion.62
  312.6 13.9 reshape.181
  326.5 12.6 copy.101
  339.1 13.9 reshape.180
  352.9 12.6 copy.100
  365.5 13.9 reshape.179
  379.4 12.8 copy.99
  398.1 88.5 %while.26 = (s32[]{:T(128)}, bf16[8,2,320,8,64]{2,1,0,4,3:T(2,128)(2,1)}, f32[8,2,8,320]{3,2,1,0:T(8,128)}, bf16[8,2,320,8,64]{2,4,3,1,0:T(8,128)(2,1)}, f32[8,2...) while((s32[]{:T(128)}, ...), condition=%wide.region_5.6_spmd, body=%wide.region_2.5_spmd.sunk | while | flops 439414400 | bytes 24291436 | solution.py:174
  486.6 14.3 reshape.152
  513.5 116.7 %reduce-scatter.17.cloned.1.call-done = bf16[2560,1024]{1,0:T(8,128)(2,1)} async-done(((bf16[5120,1024]{1,0:T(8,128)(2,1)}), bf16[2560,1024]{1,0:T(8,128)(2,1)}) %reduce-scatter.17.cloned.1.call-update) | async-done | bytes 5242896 | tf_op jit(solution)/shard_map/reduce_scatter | solution.py:76
  668.9 21.3 all-gather.3
  690.2 115.4 %all-to-all-done.1 = bf16[2,2560,1024]{2,1,0:T(8,128)(2,1)} async-done(((bf16[2,2560,1024]{2,1,0:T(8,128)(2,1)}), bf16[2,2560,1024]{2,1,0:T(8,128)(2,1)}, u32[]{:S(2)}, u32[]{:S(2)}) %all-to-all-start.1) | async-done | bytes 10485792 | tf_op jit(solution)/shard_map/all_to_all | solution.py:63
  805.6 42.3 %multiply_convert_fusion.3 = (bf16[5120,2048]{1,0:T(8,128)(2,1)}, f32[5120,2048]{1,0:T(8,128)}) fusion(f32[2048]{0:T(1024)S(1)} %bitcast.235, bf16[5120,1024]{1,0:T(8,128)(2,1)} %bitcast.38, bf16[1024,2048]{1,0:T(8,128)(2,1)} %all-gather.15.cloned.1.call-done), kind=kOutput, calls=%fused_computation.71 | convolution fusion | flops 21579694080 | bytes 77602816 | tf_op jit(solution)/shard_map/dot_general | solution.py:179
  847.9 42.4 %all-gather.19.cloned.1.call-done = bf16[5120,1024]{1,0:T(8,128)(2,1)} async-done(((bf16[2560,1024]{1,0:T(8,128)(2,1)}), bf16[5120,1024]{1,0:T(8,128)(2,1)}) %all-gather.19.cloned.1.call-update) | async-done | bytes 10485776 | tf_op jit(solution)/shard_map/all_gather | solution.py:68
  890.2 56.0 %fusion.100 = (bf16[2048]{0:T(1024)(128)(2,1)}, bf16[5120,2048]{1,0:T(8,128)(2,1)}) fusion(f32[5120,2048]{1,0:T(8,128)} %get-tuple-element.277, f32[2048]{0:T(1024)S(1)} %bitcast.236, bf16[5120,1024]{1,0:T(8,128)(2,1)} %all-gather.19.cloned.1.call-done, bf16[2048,1024]{0,1:T(8,128)(2,1)} %all-gather.17.cloned.1.call-done), kind=kOutput, calls=%fused_computation.153 | convolution fusion | flops 21705521152 | bytes 77606912 | tf_op jit(solution)/shard_map/dot_general | solution.py:14
  946.2 28.3 %fusion.101 = f32[5120,1024]{1,0:T(8,128)} fusion(bf16[5120,2048]{1,0:T(8,128)(2,1)} %get-tuple-element.279, bf16[1024,2048]{1,0:T(8,128)(2,1)} %all-gather.15.cloned.1.call-done), kind=kOutput, calls=%fused_computation.154 | convolution fusion | flops 21474836480 | bytes 46137344 | tf_op jit(solution)/shard_map/dot_general | solution.py:14
  974.5 27.8 %convolution_convert_fusion.1 = bf16[5120,1024]{1,0:T(8,128)(2,1)} fusion(bf16[5120,2048]{1,0:T(8,128)(2,1)} %get-tuple-element.276, bf16[2048,1024]{0,1:T(8,128)(2,1)} %all-gather.17.cloned.1.call-done), kind=kOutput, calls=%fused_computation.112 | convolution fusion | flops 21480079360 | bytes 35651584 | tf_op jit(solution)/shard_map/dot_general | solution.py:74
  1002.5 206.4 %reduce-scatter.21.cloned.1.call-done = f32[2560,1024]{1,0:T(8,128)} async-done(((f32[5120,1024]{1,0:T(8,128)}), f32[2560,1024]{1,0:T(8,128)}) %reduce-scatter.21.cloned.1.call-update) | async-done | bytes 10485776 | tf_op jit(solution)/shard_map/reduce_scatter | solution.py:93
  1219.9 113.9 %reduce-scatter.19.cloned.1.call-done = bf16[2560,1024]{1,0:T(8,128)(2,1)} async-done(((bf16[5120,1024]{1,0:T(8,128)(2,1)}), bf16[2560,1024]{1,0:T(8,128)(2,1)}) %reduce-scatter.19.cloned.1.call-update) | async-done | bytes 5242896 | tf_op jit(solution)/shard_map/reduce_scatter | solution.py:76
  1333.8 16.5 fusion.95
  1357.6 29.1 %convolution_convert_fusion.3 = bf16[2048,1024]{0,1:T(8,128)(2,1)} fusion(bf16[5120,2048]{1,0:T(8,128)(2,1)} %get-tuple-element.276, bf16[5120,1024]{1,0:T(8,128)(2,1)} %all-gather.19.cloned.1.call-done), kind=kOutput, calls=%fused_computation.118 | convolution fusion | flops 21476933632 | bytes 35651584 | tf_op jit(solution)/shard_map/dot_general | solution.py:20
  1386.8 29.3 %convolution_convert_fusion.4 = bf16[1024,2048]{1,0:T(8,128)(2,1)} fusion(bf16[5120,1024]{1,0:T(8,128)(2,1)} %bitcast.38, bf16[5120,2048]{1,0:T(8,128)(2,1)} %get-tuple-element.279), kind=kOutput, calls=%fused_computation.119 | convolution fusion | flops 21476933632 | bytes 35651584 | tf_op jit(solution)/shard_map/dot_general | solution.py:20
  1416.2 71.0 %all-gather.21.cloned.1.call-done = bf16[5120,1024]{1,0:T(8,128)(2,1)} async-done(((bf16[2560,1024]{1,0:T(8,128)(2,1)}), bf16[5120,1024]{1,0:T(8,128)(2,1)}) %all-gather.21.cloned.1.call-update) | async-done | bytes 10485776 | tf_op jit(solution)/shard_map/all_gather | solution.py:68
  1498.5 14.0 reshape.170
  1512.6 12.6 copy.106
  1531.0 177.5 %while.27 = (s32[]{:T(128)}, bf16[8,2,320,8,64]{2,4,3,1,0:T(8,128)(2,1)}, bf16[8,2,320,8,64]{2,1,0,4,3:T(2,128)(2,1)}, bf16[8,2,320,8,64]{2,4,3,1,0:T(8,128)(2,1...) while((s32[]{:T(128)}, ...), condition=%wide.region_15.16_spmd, body=%wide.region_13.15_spmd.sunk | while | flops 1074785920 | bytes 58479748 | solution.py:199
  1708.5 12.7 copy.110
  1725.1 13.1 copy.108
  1742.9 14.3 stack_reshape.9
  1757.2 14.3 stack_reshape.11
  1771.5 14.3 stack_reshape.10
  1785.9 22.5 convert_bitcast_fusion
  1814.2 14.5 reshape.155
  1828.7 14.3 reshape.157
  1843.0 14.3 reshape.156
  1868.3 12.9 fusion.91
  1881.2 12.7 fusion.92
  1893.9 23.9 add_add_fusion
  1920.3 34.7 %all-reduce.1 = bf16[2048]{0:T(1024)(128)(2,1)S(1)} all-reduce(bf16[2048]{0:T(1024)(128)(2,1)S(1)} %copy-done.26), channel_id=11, replica_groups=mesh['dp'=16,'tensor'=2] {'dp'}, use_global_device_ids=true, to_apply=%region_27.28.clone | all-reduce | flops 2048 | bytes 8192
  1962.4 53.9 %reduce-scatter.25.cloned.1.call-done = bf16[512,64]{0,1:T(8,128)(2,1)} async-done(((bf16[512,1024]{0,1:T(8,128)(2,1)}), bf16[512,64]{0,1:T(8,128)(2,1)}) %reduce-scatter.25.cloned.1.call-update) | async-done | bytes 65552 | tf_op jit(solution)/shard_map/reduce_scatter | solution.py:222
  2017.8 234.0 %reduce-scatter.23.cloned.1.call-done = f32[2560,1024]{1,0:T(8,128)} async-done(((f32[5120,1024]{1,0:T(8,128)}), f32[2560,1024]{1,0:T(8,128)}) %reduce-scatter.23.cloned.1.call-update) | async-done | bytes 10485776 | tf_op jit(solution)/shard_map/reduce_scatter | solution.py:93
  2262.1 14.1 fusion.80
  2276.2 120.6 %reduce-scatter.33.cloned.1.call-done = f32[32,2]{1,0:T(8,128)} async-done(((f32[1024,2]{1,0:T(8,128)}), f32[32,2]{1,0:T(8,128)}) %reduce-scatter.33.cloned.1.call-update) | async-done | bytes 272
  2398.2 132.5 %reduce-scatter.35.cloned.1.call-done = f32[32,4]{1,0:T(8,128)} async-done(((f32[1024,4]{1,0:T(8,128)}), f32[32,4]{1,0:T(8,128)}) %reduce-scatter.35.cloned.1.call-update) | async-done | bytes 528
  (309 shorter events, 447.1 us)
Async XLA Ops:
  7.2 8.0 copy-start.30
  7.2 78.3 %copy-start.27 = (f32[4,32]{1,0:T(4,128)S(1)}, f32[4,32]{1,0:T(4,128)}, u32[]{:S(2)}) copy-start(f32[4,32]{1,0:T(4,128)} %param.25) | copy-start | bytes 1540
  7.2 279.6 %all-gather.11.cloned.1.call-start = ((), (), s32[]{:S(2)}) async-start(), calls=%async_computation.12 | async-start | bytes 3342336 | tf_op jit(solution)/shard_map/all_gather | solution.py:43
  11.2 155.2 %copy-start.3 = (f32[2560]{0:T(1024)}, f32[2560]{0:T(1024)S(1)}, u32[]{:S(2)}) copy-start(f32[2560]{0:T(1024)S(1)} %broadcast_multiply_fusion.5) | copy-start | bytes 30724
  15.2 151.2 %copy-start.7 = (f32[2560]{0:T(1024)}, f32[2560]{0:T(1024)S(1)}, u32[]{:S(2)}) copy-start(f32[2560]{0:T(1024)S(1)} %add_rsqrt_fusion.1) | copy-start | bytes 30724
  150.4 16.0 copy-start.16
  166.4 8.6 copy-start.34
  166.4 9.1 copy-start.31
  166.5 120.3 %all-to-all-start = ((bf16[2,2560,1024]{2,1,0:T(8,128)(2,1)}), bf16[2,2560,1024]{2,1,0:T(8,128)(2,1)}, u32[]{:S(2)}, u32[]{:S(2)}) async-start(bf16[2,2560,1024]{2,1,0:T(8,128)(2,1)} %pad_maximum_fusion), calls=%async_computation | async-start | bytes 20971520 | tf_op jit(solution)/shard_map/all_to_all | solution.py:63
  174.2 326.8 %all-gather.13.cloned.1.call-start = ((), (), s32[]{:S(2)}) async-start(), calls=%async_computation.13 | async-start | bytes 1114112 | tf_op jit(solution)/shard_map/all_gather | solution.py:44
  174.9 455.4 %reduce-scatter.17.cloned.1.call-start = ((), (), s32[]{:S(2)}) async-start(), calls=%async_computation.14 | async-start | bytes 15728640 | tf_op jit(solution)/shard_map/reduce_scatter | solution.py:76
  486.6 25.5 %copy-start.13 = (f32[8,2,320]{2,1,0:T(2,128)}, f32[8,2,320]{2,1,0:T(2,128)S(1)}, u32[]{:S(2)}) copy-start(f32[8,2,320]{2,1,0:T(2,128)S(1)} %get-tuple-element.514) | copy-start | bytes 61444
  512.1 118.2 %copy-start.11 = (f32[1,1024]{1,0:T(1,128)S(1)}, f32[1,1024]{1,0:T(1,128)}, u32[]{:S(2)}) copy-start(f32[1,1024]{1,0:T(1,128)} %get-tuple-element.270) | copy-start | bytes 12292
  512.1 124.2 %slice-start = ((s8[5242880]{0:T(1024)(128)(4,1)}), s8[1048576]{0:T(1024)(128)(4,1)S(1)}, s32[]{:S(2)}) async-start(s8[5242880]{0:T(1024)(128)(4,1)} %bitcast.204), calls=%async_computation.29 | async-start | bytes 2097152
  512.1 178.0 %all-gather.15.cloned.1.call-start = ((), (), s32[]{:S(2)}) async-start(), calls=%async_computation.15 | async-start | bytes 4456448 | tf_op jit(solution)/shard_map/all_gather | solution.py:45
  512.7 335.1 %all-gather.17.cloned.1.call-start = ((), (), s32[]{:S(2)}) async-start(), calls=%async_computation.16 | async-start | bytes 4456448 | tf_op jit(solution)/shard_map/all_gather | solution.py:46
  513.5 149.4 %copy-start.14 = (f32[2560]{0:T(1024)}, f32[2560]{0:T(1024)S(1)}, u32[]{:S(2)}) copy-start(f32[2560]{0:T(1024)S(1)} %dynamic_slice.36) | copy-start | bytes 30724
  630.3 6.8 slice-start.1
  630.3 11.0 copy-start.18
  630.3 11.0 copy-start.22
  655.0 150.6 %all-to-all-start.1 = ((bf16[2,2560,1024]{2,1,0:T(8,128)(2,1)}), bf16[2,2560,1024]{2,1,0:T(8,128)(2,1)}, u32[]{:S(2)}, u32[]{:S(2)}) async-start(bf16[2,2560,1024]{2,1,0:T(8,128)(2,1)} %pad_maximum_fusion.1), calls=%async_computation.2 | async-start | bytes 20971520 | tf_op jit(solution)/shard_map/all_to_all | solution.py:63
  662.9 227.3 %all-gather.19.cloned.1.call-start = ((), (), s32[]{:S(2)}) async-start(), calls=%async_computation.18 | async-start | bytes 15728640 | tf_op jit(solution)/shard_map/all_gather | solution.py:68
  668.8 540.1 %reduce-scatter.21.cloned.1.call-start = ((), (), s32[]{:S(2)}) async-start(), calls=%async_computation.19 | async-start | bytes 31457280 | tf_op jit(solution)/shard_map/reduce_scatter | solution.py:93
  974.5 359.3 %reduce-scatter.19.cloned.1.call-start = ((), (), s32[]{:S(2)}) async-start(), calls=%async_computation.17 | async-start | bytes 15728640 | tf_op jit(solution)/shard_map/reduce_scatter | solution.py:76
  1002.4 206.6 %copy-start.6 = (f32[2560]{0:T(1024)S(1)}, f32[2560]{0:T(1024)}, u32[]{:S(2)}) copy-start(f32[2560]{0:T(1024)} %copy-done.5) | copy-start | bytes 30724
  1002.4 206.6 %copy-start.10 = (f32[2560]{0:T(1024)S(1)}, f32[2560]{0:T(1024)}, u32[]{:S(2)}) copy-start(f32[2560]{0:T(1024)} %copy-done.9) | copy-start | bytes 30724
  1002.4 206.6 %copy-start.12 = (f32[1,1024]{1,0:T(1,128)S(1)}, f32[1,1024]{1,0:T(1,128)}, u32[]{:S(2)}) copy-start(f32[1,1024]{1,0:T(1,128)} %get-tuple-element.270) | copy-start | bytes 12292
  1002.4 206.6 %copy-start.19 = (f32[1,1024]{1,0:T(1,128)S(1)}, f32[1,1024]{1,0:T(1,128)}, u32[]{:S(2)}) copy-start(f32[1,1024]{1,0:T(1,128)} %get-tuple-element.273) | copy-start | bytes 12292
  1002.4 331.4 %copy-start.15 = (f32[2560]{0:T(1024)S(1)}, f32[2560]{0:T(1024)}, u32[]{:S(2)}) copy-start(f32[2560]{0:T(1024)} %copy-done.14) | copy-start | bytes 30724
  1002.4 331.4 %copy-start.25 = (f32[1,1024]{1,0:T(1,128)S(1)}, f32[1,1024]{1,0:T(1,128)}, u32[]{:S(2)}) copy-start(f32[1,1024]{1,0:T(1,128)} %get-tuple-element.268) | copy-start | bytes 12292
  1002.5 484.8 %all-gather.21.cloned.1.call-start = ((), (), s32[]{:S(2)}) async-start(), calls=%async_computation.20 | async-start | bytes 15728640 | tf_op jit(solution)/shard_map/all_gather | solution.py:68
  1357.6 598.0 %reduce-scatter.29.cloned.1.call-start = ((), (), s32[]{:S(2)}) async-start(), calls=%async_computation.24 | async-start | bytes 4456448 | tf_op jit(solution)/shard_map/reduce_scatter | solution.py:228
  1386.8 570.6 %reduce-scatter.27.cloned.1.call-start = ((), (), s32[]{:S(2)}) async-start(), calls=%async_computation.23 | async-start | bytes 4456448 | tf_op jit(solution)/shard_map/reduce_scatter | solution.py:225
  1386.8 100.4 %copy-start.33 = (bf16[512,1024]{0,1:T(8,128)(2,1)S(1)}, bf16[512,1024]{0,1:T(8,128)(2,1)}, u32[]{:S(2)}) copy-start(bf16[512,1024]{0,1:T(8,128)(2,1)} %all-gather.13.cloned.1.call-done) | copy-start | bytes 3145732
  1416.2 543.0 %reduce-scatter.31.cloned.1.call-start = ((), (), s32[]{:S(2)}) async-start(), calls=%async_computation.25 | async-start | bytes 139264
  1785.8 174.7 %all-reduce.4.cloned.1.call-start = ((), (), s32[]{:S(2)}) async-start(), calls=%async_computation.28 | async-start | bytes 8388608
  1814.1 202.2 %reduce-scatter.25.cloned.1.call-start = ((), (), s32[]{:S(2)}) async-start(), calls=%async_computation.22 | async-start | bytes 1114112 | tf_op jit(solution)/shard_map/reduce_scatter | solution.py:222
  1857.3 11.0 copy-start.2
  1868.3 383.6 %reduce-scatter.23.cloned.1.call-start = ((), (), s32[]{:S(2)}) async-start(), calls=%async_computation.21 | async-start | bytes 31457280 | tf_op jit(solution)/shard_map/reduce_scatter | solution.py:93
  1917.8 334.0 %copy-start.4 = (f32[2560]{0:T(1024)S(1)}, f32[2560]{0:T(1024)}, u32[]{:S(2)}) copy-start(f32[2560]{0:T(1024)} %copy-done.3) | copy-start | bytes 30724
  1917.8 334.0 %copy-start.8 = (f32[2560]{0:T(1024)S(1)}, f32[2560]{0:T(1024)}, u32[]{:S(2)}) copy-start(f32[2560]{0:T(1024)} %copy-done.7) | copy-start | bytes 30724
  1917.8 334.0 %copy-start.17 = (f32[1,1024]{1,0:T(1,128)S(1)}, f32[1,1024]{1,0:T(1,128)}, u32[]{:S(2)}) copy-start(f32[1,1024]{1,0:T(1,128)} %copy-done.16) | copy-start | bytes 12292
  1917.8 342.0 %copy-start.20 = (f32[1024]{0:T(1024)S(1)}, f32[1024]{0:T(1024)}, u32[]{:S(2)}) copy-start(f32[1024]{0:T(1024)} %get-tuple-element.215) | copy-start | bytes 12292
  1917.8 343.1 %copy-start.21 = (f32[1024]{0:T(1024)S(1)}, f32[1024]{0:T(1024)}, u32[]{:S(2)}) copy-start(f32[1024]{0:T(1024)} %get-tuple-element.222) | copy-start | bytes 12292
  1917.9 343.1 %copy-start.23 = (f32[1024]{0:T(1024)S(1)}, f32[1024]{0:T(1024)}, u32[]{:S(2)}) copy-start(f32[1024]{0:T(1024)} %get-tuple-element.257) | copy-start | bytes 12292
  1917.9 343.1 %copy-start.24 = (f32[1024]{0:T(1024)S(1)}, f32[1024]{0:T(1024)}, u32[]{:S(2)}) copy-start(f32[1024]{0:T(1024)} %get-tuple-element.267) | copy-start | bytes 12292
  1917.9 478.9 %reduce-scatter.33.cloned.1.call-start = ((), (), s32[]{:S(2)}) async-start(), calls=%async_computation.26 | async-start | bytes 540672
  2260.9 269.7 %reduce-scatter.35.cloned.1.call-start = ((), (), s32[]{:S(2)}) async-start(), calls=%async_computation.27 | async-start | bytes 540672
  (9 other events, 25.2 us)
Sparse Core Ops, SparseCore 0:
  10.2 48.2 all-gather.10
  177.2 35.8 all-gather.12
  512.2 117.9 reduce-scatter.16
  632.3 50.3 all-gather.14
  684.7 48.8 all-gather.16
  735.6 154.5 all-gather.18
  974.6 234.2 reduce-scatter.20
  1211.8 121.9 reduce-scatter.18
  1357.7 129.4 all-gather.20
  1490.9 72.9 reduce-scatter.28
  1567.8 71.5 reduce-scatter.26
  1785.9 55.8 reduce-scatter.30
  1845.5 110.4 all-reduce.3
  1959.5 56.7 reduce-scatter.24
  2018.5 233.3 reduce-scatter.22
  2261.1 135.7 reduce-scatter.32
  2398.9 131.6 reduce-scatter.34
